TPU v7x, 512 devices: a whole 4x8x8 slice. The times are simulated.
512 devices in a mesh: grp: 16 (over x_lo, y), blk: 32 (over x_hi, z, core).
Axes of the slice: x: 4 (x_hi: 2, x_lo: 2; x = x_hi * 2 + x_lo), y: 8, z: 8, core: 2. Of those that a mesh axis runs over, the one named last changes fastest.
Arguments:
- walkers: bfloat16 [128, 128, 768], P('blk', 'grp'), may hold values from -6 to 6
- one_body: bfloat16 [768, 768], replicated, may hold values from -0.21875 to 0.21875
- fields: float32 [128, 384], P('grp', 'blk'), may hold values from -6 to 6
- field_diag: float32 [384, 768], P('blk'), may hold values from -0.4375 to 0.4375
- chol: bfloat16 [384, 128, 768], P('blk'), may hold values from -0.1875 to 0.1875
- weights: float32 [128], P('grp'), may hold values from 0.25 to 12, as said below
- target: int32 [128], P('grp'), may hold values from 0 to 64, as said below
Outputs:
- fock: bfloat16 [128, 128, 768], P('blk', 'grp')
Inputs may be any that keep to these rules, and one draw needn't show every extreme that they name: `target`: each list of 8 slots (the slots of one index of grp) holds its live walkers in its first slots. The live walkers of all lists, in order of list and slot, carry the numbers 0 to 63, each once; a dead slot holds 64. A list holds 0 to 8 live walkers, and some list holds exactly 8. `weights`: Positive.
All inputs are finite; a program needn't handle non-finite values.
Results may differ from a plain program's by a relative error of at most 0.018.
Values may be sent and summed in bfloat16 or wider, within the bound.
A program may use at most 64 MiB of HBM per device.

v0:
```python
import jax
import jax.numpy as jnp
from jax import lax
from jax.sharding import PartitionSpec as P


def measure(blocks, chol):
    vec_count = chol.shape[0]
    occupied = chol.shape[1]
    vectors = chol.reshape(-1, chol.shape[2])
    portion = lax.all_gather(blocks, "blk", axis=0, tiled=True)
    flat = portion.reshape(-1, portion.shape[2])
    result = lax.dot_general(
        vectors, flat, (((1,), (1,)), ((), ())), preferred_element_type=jnp.float32
    )
    result = result.reshape(vec_count, occupied, portion.shape[0], portion.shape[1])
    coupling = jnp.transpose(result, (1, 3, 0, 2)).astype(jnp.bfloat16)
    amount = blocks.shape[0] * lax.axis_size("blk")
    result = jnp.dot(
        coupling.reshape(amount * coupling.shape[1], -1),
        vectors,
        preferred_element_type=jnp.float32,
    )
    return lax.psum_scatter(
        result.reshape(amount, coupling.shape[1], -1).astype(jnp.bfloat16),
        "blk",
        scatter_dimension=0,
        tiled=True,
    ).astype(jnp.float32)


def body(walkers, one_body, fields, field_diag, chol, weights, target):
    slot_count = walkers.shape[1]
    orbitals = walkers.shape[2]
    field_part = jnp.dot(fields, field_diag, precision=lax.Precision.HIGHEST)
    exponent = lax.psum(field_part, "blk")
    scaled = (walkers.astype(jnp.float32) * jnp.exp(exponent)[None]).astype(jnp.bfloat16)
    propagated = jnp.dot(scaled.reshape(-1, orbitals), one_body, preferred_element_type=jnp.float32)
    propagated = propagated.astype(jnp.bfloat16).reshape(walkers.shape)
    live_total = slot_count // 2 * lax.axis_size("grp")
    active = target < live_total
    weight_sum = lax.psum(jnp.sum(jnp.where(active, weights, jnp.float32(0.0))), "grp")
    factor = jnp.where(active, weights * live_total / weight_sum, jnp.float32(0.0))
    fock_raw = lax.optimization_barrier(measure(propagated, chol).astype(jnp.bfloat16)).astype(
        jnp.float32
    )
    return (fock_raw * factor[None, :, None]).astype(jnp.bfloat16)


def solution(mesh):
    in_specs = (
        P("blk", "grp", None),
        P(),
        P("grp", "blk"),
        P("blk", None),
        P("blk", None, None),
        P("grp"),
        P("grp"),
    )
    out_specs = P("blk", "grp", None)
    return jax.shard_map(body, mesh=mesh, in_specs=in_specs, out_specs=out_specs, check_vma=False)
```

profile of v0, /device:TPU:1, one launch (start us, length us, event | category | flops | bytes accessed | tf_op | source)
XLA Modules:
  0.0 372.2 jit_solution(6693121120049751304)
XLA Ops:
  6.5 0.0 copy-start
  6.5 0.0 all-gather.2.cloned.1.call-start
  6.5 1.1 fusion.14
  7.7 134.9 %psum.14 = f32[8,768]{1,0:T(8,128)S(1)} all-reduce(f32[8,768]{1,0:T(8,128)S(1)} %fusion.14), channel_id=1, replica_groups=mesh['grp'=16,'blk'=32] {'blk'}, use_global_device_ids=true, to_apply=%region_0.0 | all-reduce | flops 6144 | bytes 49152 | tf_op jit(solution)/shard_map/psum | solution.py:36
  142.6 2.2 fusion.9
  144.9 0.0 all-gather.2.cloned.1.call-update
  144.9 0.0 reduce-scatter.2.cloned.1.call-start
  144.9 84.8 %all-gather.2.cloned.1.call-done = bf16[128,8,768]{2,1,0:T(8,128)(2,1)} async-done(((bf16[4,8,768]{2,1,0:T(8,128)(2,1)}), bf16[128,8,768]{2,1,0:T(8,128)(2,1)}) %all-gather.2.cloned.1.call-update) | async-done | bytes 1572880 | tf_op jit(solution)/shard_map/all_gather | solution.py:11
  229.7 0.0 copy-done
  229.7 5.5 %fusion.3 = bf16[12,128,128,8]{1,3,0,2:T(8,128)(2,1)} fusion(bf16[1536,768]{1,0:T(8,128)(2,1)S(1)} %bitcast.30, bf16[128,8,768]{2,1,0:T(8,128)(2,1)} %all-gather.2.cloned.1.call-done), kind=kOutput, calls=%fused_computation.5 | convolution fusion | flops 2417491968 | bytes 7077888 | tf_op jit(solution)/shard_map/dot_general | solution.py:13
  235.2 5.0 %copy.10 = bf16[12,128,128,8]{2,1,0,3:T(8,128)(2,1)} copy(bf16[12,128,128,8]{1,3,0,2:T(8,128)(2,1)} %fusion.3) | data formatting | bytes 6291456 | tf_op jit(solution)/shard_map/convert_element_type | solution.py:17
  240.1 4.2 %bitcast_convert_fusion = bf16[128,8,768]{2,0,1:T(8,128)(2,1)S(1)} fusion(bf16[12,128,768]{2,1,0:T(8,128)(2,1)S(1)} %copy-done, bf16[12,128,128,8]{2,1,0,3:T(8,128)(2,1)} %copy.10), kind=kOutput, calls=%fused_computation.1 | convolution fusion | flops 2416705536 | bytes 7077888 | tf_op jit(solution)/shard_map/dot_general | solution.py:19
  244.4 0.0 copy-start.1
  244.4 0.0 copy-start.2
  244.4 2.0 copy.11
  246.4 0.0 reduce-scatter.2.cloned.1.call-update
  246.4 0.0 copy-done.1
  246.5 0.0 copy-done.2
  246.5 0.6 fusion.13
  247.1 27.1 %psum.15 = f32[]{:T(128)} all-reduce(f32[]{:T(128)} %fusion.13), channel_id=1, replica_groups=mesh['grp'=16,'blk'=32] {'grp'}, use_global_device_ids=true, to_apply=%region_3.4 | all-reduce | flops 1 | bytes 8 | tf_op jit(solution)/shard_map/psum | solution.py:42
  274.1 0.7 compare_select_fusion
  274.8 89.0 %reduce-scatter.2.cloned.1.call-done = bf16[4,8,768]{2,1,0:T(8,128)(2,1)} async-done(((bf16[128,8,768]{2,1,0:T(8,128)(2,1)}), bf16[4,8,768]{2,1,0:T(8,128)(2,1)}) %reduce-scatter.2.cloned.1.call-update) | async-done | bytes 49168 | tf_op jit(solution)/shard_map/reduce_scatter | solution.py:24
  363.8 1.5 multiply_convert_fusion
  (1 shorter events, 0.0 us)
Async XLA Ops:
  6.5 223.2 %copy-start = (bf16[12,128,768]{2,1,0:T(8,128)(2,1)S(1)}, bf16[12,128,768]{2,1,0:T(8,128)(2,1)}, u32[]{:S(2)}) copy-start(bf16[12,128,768]{2,1,0:T(8,128)(2,1)} %param.11) | copy-start | bytes 7077892
  6.5 223.2 %all-gather.2.cloned.1.call-start = ((), (), s32[]{:S(2)}) async-start(), calls=%async_computation.1 | async-start | bytes 1622016 | tf_op jit(solution)/shard_map/all_gather | solution.py:11
  144.9 218.9 %reduce-scatter.2.cloned.1.call-start = ((), (), s32[]{:S(2)}) async-start(), calls=%async_computation.2 | async-start | bytes 1622016 | tf_op jit(solution)/shard_map/reduce_scatter | solution.py:24
  244.4 2.1 copy-start.1
  244.4 2.1 copy-start.2
Sparse Core Ops, SparseCore 0:
  145.0 84.6 all-gather.1
  246.6 117.2 reduce-scatter.1
where the time goes:
time: 377 us; the launch traced here: 372 us
  waiting for transfers between devices  174 us (46%)
  blocking collectives  162 us (43%)
  between operations  13.5 us (4%)
  matrix products  13 us (3%)
  local copies, waits for them, and re-layouts  7.02 us (2%)
    psum x1, blocking collectives, body(): exponent = lax.psum(field_part, 'blk')  135 us
    reduce_scatter x1, waiting for transfers between devices, measure(): lax.psum_scatter(result.reshape(amount, coupling.shape[1], -1).astype(jnp...  89 us
    all_gather x1, waiting for transfers between devices, measure(): portion = lax.all_gather(blocks, 'blk', axis=0, tiled=True)  84.8 us
    psum x1, blocking collectives, body(): lax.psum(jnp.sum(jnp.where(active, weights, jnp.float32(0.0))), 'grp')  27.1 us
  transfers between devices with their start and end apart: 2, of which 2 were waited for; matrix products, arithmetic and copies ran while one was open for 0% of the time, Pallas kernels for 0%

commit v1 on v0

v1 whole, which is shorter than its diff:
```python
import jax
import jax.numpy as jnp
from jax import lax
from jax.experimental import pallas as pl
from jax.experimental.pallas import tpu as pltpu
from jax.sharding import PartitionSpec as P

MESH = pl.DeviceIdType.MESH
F32 = jnp.float32
BF16 = jnp.bfloat16

NZ = 8
NY = 8
SLOTS = 8
HALF = SLOTS // 2
ROWS = 4
QUAD = 4
ZROWS = QUAD * ROWS
NOCC = NZ * ZROWS
NORB = 768
LANES = NORB // 128
VEC = 12
TV = 6
LIVE = 64


def far(walker):
    up = 4 if walker < HALF // 2 else 3
    return up, NZ - 1 - up


def kernel(
    walkers, one_body, fields, field_diag, chol, weights, target, out,
    X, S, G, FI, FD, EP, ER, E, ET, OB, CH, PR, LH, F, RS, RR, T, PC, FR, O, OW, WS, WX, WR,
    loc, qs, qr, es, er, ws, wr, gs, gr, ss, sr, fs, fr,
):
    p = lax.axis_index("grp")
    b = lax.axis_index("blk")
    x_lo, y = p // NY, p % NY
    x_hi, z, c = b // (2 * NZ), (b // 2) % NZ, b % 2
    q_me = x_hi * 2 + c

    def at_blk(xh, zz, cc):
        return {"blk": xh * (2 * NZ) + zz * 2 + cc}

    quad = {
        k: at_blk(x_hi ^ 1 if k & 2 else x_hi, z, c ^ 1 if k & 1 else c) for k in (1, 2, 3)
    }
    z_dev = (at_blk(x_hi, (z + 1) % NZ, c), at_blk(x_hi, (z + NZ - 1) % NZ, c))
    y_dev = ({"grp": x_lo * NY + (y + 1) % NY}, {"grp": x_lo * NY + (y + NY - 1) % NY})
    x_dev = {"grp": (x_lo ^ 1) * NY + y}

    def rcopy(src, dst, s, r, dev):
        return pltpu.make_async_remote_copy(
            src_ref=src, dst_ref=dst, send_sem=s, recv_sem=r, device_id=dev, device_id_type=MESH
        )

    local = [
        pltpu.make_async_copy(fields, FI, loc.at[0]),
        pltpu.make_async_copy(field_diag, FD, loc.at[1]),
        pltpu.make_async_copy(walkers, X.at[q_me], loc.at[2]),
        pltpu.make_async_copy(one_body, OB, loc.at[3]),
        pltpu.make_async_copy(chol.at[:, 0], CH.at[pl.ds(0, VEC), :, 0], loc.at[4]),
        pltpu.make_async_copy(chol.at[:, 1], CH.at[pl.ds(0, VEC), :, 1], loc.at[5]),
    ]
    for copy in local:
        copy.start()

    barrier = pltpu.get_barrier_semaphore()
    partners = list(quad.values()) + list(z_dev) + list(y_dev) + [x_dev]
    for dev in partners:
        pl.semaphore_signal(barrier, inc=1, device_id=dev, device_id_type=MESH)

    local[0].wait()
    local[1].wait()
    part = FI[:, 0:1] * FD[0:1, :]
    for k in range(1, VEC):
        part += FI[:, k : k + 1] * FD[k : k + 1, :]
    EP[0] = part[:HALF]
    EP[1] = part[HALF:]

    own = jnp.float32(0.0)
    for s in range(SLOTS):
        own = own + jnp.where(target[s] < LIVE, weights[s], jnp.float32(0.0))
    WS[...] = jnp.full((8, 128), own, F32)

    pl.semaphore_wait(barrier, len(partners))

    e_quad = [rcopy(EP.at[c ^ 1 if k & 1 else c], ER.at[k - 1], es.at[k - 1], er.at[k - 1], quad[k]) for k in (2, 3, 1)]
    x_quad = [rcopy(walkers, X.at[q_me], qs.at[k - 1], qr.at[k - 1], quad[k]) for k in (2, 3, 1)]
    for copy in e_quad + x_quad:
        copy.start()
    w_pair = rcopy(WS, WX, ws.at[0], wr.at[0], x_dev)
    w_pair.start()
    c_pair = [
        rcopy(chol.at[:, h], CH.at[pl.ds(VEC, VEC), :, h], fs.at[h], fr.at[h], quad[1])
        for h in range(2)
    ]
    for copy in c_pair:
        copy.start()

    def item(view, me, devs, send, recv, steps):
        def block(way, hop):
            return (me - hop) % 8 if way == 0 else (me + hop) % 8

        def copy(way, step):
            ref = view(block(way, step - 1))
            return rcopy(ref, ref, send.at[way, step - 1], recv.at[way, step - 1], devs[way])

        def arrived(way, step):
            ref = view(block(way, step))
            rcopy(ref, ref, send.at[way, step - 1], recv.at[way, step - 1], devs[way]).wait_recv()

        return copy, arrived, steps

    items = [item(lambda i: E.at[i], z, z_dev, gs.at[HALF], gr.at[HALF], (4, 3))]
    for w in range(HALF):
        items.append(item(lambda i, w=w: G.at[w, i], z, z_dev, gs.at[w], gr.at[w], far(w)))
    items.append(item(lambda i: WR.at[i], y, y_dev, gs.at[HALF + 1], gr.at[HALF + 1], (4, 3)))
    sent = []

    def start(it, step):
        copy, _, steps = it
        for way in range(2):
            if step <= steps[way]:
                cp = copy(way, step)
                cp.start()
                sent.append(cp)

    def forward(it, step):
        copy, arrived, steps = it
        for way in range(2):
            if step <= steps[way]:
                arrived(way, step)
                if step + 1 <= steps[way]:
                    cp = copy(way, step + 1)
                    cp.start()
                    sent.append(cp)

    for copy in e_quad:
        copy.wait_recv()
    E[z] = (EP[c] + ER[1]) + (ER[0] + ER[2])
    start(items[0], 1)

    local[2].wait()
    for copy in x_quad:
        copy.wait_recv()
    for q in range(QUAD):
        for r in range(ROWS):
            rows = X[q, r].astype(F32)
            for n in range(LANES):
                S[n, pl.ds((q * ROWS + r) * SLOTS, SLOTS), :] = rows[:, n * 128 : (n + 1) * 128]
    for w in range(HALF):
        for n in range(LANES):
            lo = S[n, pl.ds(w, ZROWS, stride=SLOTS), :]
            hi = S[n, pl.ds(HALF + w, ZROWS, stride=SLOTS), :]
            G[w, z, :, n * 128 : (n + 1) * 128] = jnp.where(c == 0, lo, hi).astype(BF16)
        start(items[1 + w], 1)

    w_pair.wait_recv()
    WR[y] = WS[...] + WX[...]
    start(items[-1], 1)

    for step in range(1, 5):
        for it in items:
            forward(it, step)

    total = E[0]
    for i in range(1, NZ):
        total += E[i]
    ET[...] = jnp.exp(total)

    total = WR[0]
    for i in range(1, NY):
        total += WR[i]
    row = lax.broadcasted_iota(jnp.int32, (8, 128), 0)
    factor = jnp.zeros((8, 128), F32)
    for s in range(SLOTS):
        mine = jnp.where(target[s] < LIVE, weights[s] * LIVE, jnp.float32(0.0))
        factor = jnp.where(row == s, mine, factor)
    WS2 = factor / total

    local[3].wait()
    for copy in local[4:]:
        copy.wait()
    for copy in c_pair:
        copy.wait_recv()

    vectors = CH.reshape(2 * VEC * NOCC, NORB)

    rs_sent = []

    def rs_step(w, step):
        for way in range(2):
            depth = far(w)[way]
            if step > depth:
                continue
            hop = depth - step + 1
            zz = (z + hop) % NZ if way == 0 else (z + NZ - hop) % NZ
            rows = F[pl.ds(pl.multiple_of(w * NOCC + zz * ZROWS, ZROWS), ZROWS), :]
            if step > 1:
                slot = RR.at[w, way, step - 2]
                rcopy(slot, slot, ss.at[w, way, step - 2], sr.at[w, way, step - 2], z_dev[way]).wait_recv()
                rows = rows + RR[w, way, step - 2].astype(F32)
            RS[w, way, step - 1] = rows.astype(BF16)
            cp = rcopy(
                RS.at[w, way, step - 1], RR.at[w, way, step - 1],
                ss.at[w, way, step - 1], sr.at[w, way, step - 1], z_dev[way],
            )
            cp.start()
            rs_sent.append(cp)

    def compute(pair, hooks):
        base = pair * 2 * NOCC
        for w in range(2):
            wk = pair * 2 + w
            rows = G[wk].reshape(NOCC, NORB).astype(F32) * ET[wk : wk + 1, :]
            PR[w * NOCC : (w + 1) * NOCC, :] = rows.astype(BF16)
        prop = jnp.dot(PR[...], OB[...], preferred_element_type=F32).astype(BF16)
        PR[...] = prop
        for t in range(2 * VEC // TV):
            res = lax.dot_general(
                vectors[t * TV * NOCC : (t + 1) * TV * NOCC, :], PR[...],
                (((1,), (1,)), ((), ())), preferred_element_type=F32,
            ).astype(BF16)
            for g in range(TV):
                for w in range(2):
                    LH[w * NOCC : (w + 1) * NOCC, (t * TV + g) * NOCC : (t * TV + g + 1) * NOCC] = res[
                        g * NOCC : (g + 1) * NOCC, w * NOCC : (w + 1) * NOCC
                    ]
            if t == 1 and hooks:
                hooks.pop(0)()
        if hooks:
            hooks.pop(0)()
        for n in range(NORB // 256):
            F[base : base + 2 * NOCC, n * 256 : (n + 1) * 256] = jnp.dot(
                LH[...], vectors[:, n * 256 : (n + 1) * 256], preferred_element_type=F32
            )
            if n == 0 and hooks:
                hooks.pop(0)()

    def both(pair, step):
        for w in range(2):
            rs_step(pair * 2 + w, step)

    compute(0, [])
    both(0, 1)
    compute(1, [lambda s=s: both(0, s) for s in (2, 3, 4)])
    both(1, 1)
    for step in (2, 3, 4):
        both(1, step)

    for w in range(HALF):
        rows = F[pl.ds(pl.multiple_of(w * NOCC + z * ZROWS, ZROWS), ZROWS), :]
        for way in range(2):
            last = far(w)[way] - 1
            slot = RR.at[w, way, last]
            rcopy(slot, slot, ss.at[w, way, last], sr.at[w, way, last], z_dev[way]).wait_recv()
            rows = rows + RR[w, way, last].astype(F32)
        for n in range(LANES):
            T[n, w * ZROWS : (w + 1) * ZROWS, :] = rows[:, n * 128 : (n + 1) * 128]
    for q in range(QUAD):
        for r in range(ROWS):
            for n in range(LANES):
                PC[q, r, :, n * 128 : (n + 1) * 128] = T[
                    n, pl.ds(q * ROWS + r, HALF, stride=ZROWS), :
                ].astype(BF16)
    fin = [rcopy(PC.at[q_me ^ k], FR.at[k - 1], fs.at[1 + k], fr.at[1 + k], quad[k]) for k in (3, 2, 1)]
    for copy in fin:
        copy.start()
    for copy in fin:
        copy.wait_recv()
    O[c] = PC[q_me].astype(F32) + FR[1].astype(F32)
    O[c ^ 1] = FR[0].astype(F32) + FR[2].astype(F32)
    scale = WS2[:, 0:1]
    for r in range(ROWS):
        OW[r, 0:HALF, :] = O[0, r]
        OW[r, HALF:SLOTS, :] = O[1, r]
        out[r] = (OW[r].astype(BF16).astype(F32) * scale).astype(BF16)

    for copy in e_quad + x_quad + [w_pair] + c_pair + sent + rs_sent + fin:
        copy.wait_send()


def body(walkers, one_body, fields, field_diag, chol, weights, target):
    vmem, sem = pltpu.VMEM, pltpu.SemaphoreType.DMA
    any_, smem = pl.BlockSpec(memory_space=pl.ANY), pl.BlockSpec(memory_space=pltpu.SMEM)
    return pl.pallas_call(
        kernel,
        out_shape=jax.ShapeDtypeStruct((ROWS, SLOTS, NORB), BF16),
        in_specs=[any_] * 5 + [smem] * 2,
        out_specs=pl.BlockSpec(memory_space=pltpu.VMEM),
        scratch_shapes=[
            vmem((QUAD, ROWS, SLOTS, NORB), BF16),
            vmem((LANES, QUAD * ROWS * SLOTS, 128), F32),
            vmem((HALF, NZ, ZROWS, NORB), BF16),
            vmem((SLOTS, VEC), F32),
            vmem((VEC, NORB), F32),
            vmem((2, HALF, NORB), F32),
            vmem((3, HALF, NORB), F32),
            vmem((NZ, HALF, NORB), F32),
            vmem((HALF, NORB), F32),
            vmem((NORB, NORB), BF16),
            vmem((2 * VEC, NZ, 2, 8, NORB), BF16),
            vmem((2 * NOCC, NORB), BF16),
            vmem((2 * NOCC, 2 * VEC * NOCC), BF16),
            vmem((HALF * NOCC, NORB), F32),
            vmem((HALF, 2, 4, ZROWS, NORB), BF16),
            vmem((HALF, 2, 4, ZROWS, NORB), BF16),
            vmem((LANES, HALF * ZROWS, 128), F32),
            vmem((QUAD, ROWS, HALF, NORB), BF16),
            vmem((3, ROWS, HALF, NORB), BF16),
            vmem((2, ROWS, HALF, NORB), F32),
            vmem((ROWS, SLOTS, NORB), F32),
            vmem((8, 128), F32),
            vmem((8, 128), F32),
            vmem((NY, 8, 128), F32),
            sem((6,)),
            sem((3,)), sem((3,)),
            sem((3,)), sem((3,)),
            sem((1,)), sem((1,)),
            sem((HALF + 2, 2, 4)), sem((HALF + 2, 2, 4)),
            sem((HALF, 2, 4)), sem((HALF, 2, 4)),
            sem((5,)), sem((5,)),
        ],
        compiler_params=pltpu.CompilerParams(
            collective_id=0, has_side_effects=True, vmem_limit_bytes=56 * 1024 * 1024
        ),
    )(
        walkers, one_body, fields, field_diag,
        chol.reshape(VEC, 2, NZ, 8, NORB), weights, target,
    )


def solution(mesh):
    in_specs = (
        P("blk", "grp", None),
        P(),
        P("grp", "blk"),
        P("blk", None),
        P("blk", None, None),
        P("grp"),
        P("grp"),
    )
    out_specs = P("blk", "grp", None)
    return jax.shard_map(body, mesh=mesh, in_specs=in_specs, out_specs=out_specs, check_vma=False)
```

time: 377 us -> 69.4 us (0.18); the launches traced: 372 us -> 69.2 us
  waiting for transfers between devices: 174 us -> 0 us
  blocking collectives: 162 us -> 0 us
  Pallas kernels: 0 us -> 67.8 us
  between operations: 13.5 us -> 0.01 us
  matrix products: 13 us -> 0 us
  local copies, waits for them, and re-layouts: 7.02 us -> 1.42 us
    psum x2 -> x0, blocking collectives: 162 us -> none  [the longest x1 135 us: body(): exponent = lax.psum(field_part, 'blk')]
    reduce_scatter x1 -> x0, waiting for transfers between devices: 89 us -> none  [measure(): lax.psum_scatter(result.reshape(amount, coupling.shape[1], -1).astype(jnp...]
    all_gather x1 -> x0, waiting for transfers between devices: 84.8 us -> none  [measure(): portion = lax.all_gather(blocks, 'blk', axis=0, tiled=True)]
    pallas_call x0 -> x1, Pallas kernels: none -> 67.8 us  [body(): pl.pallas_call(kernel, out_shape=jax.ShapeDtypeStruct((ROWS, SLOTS, NORB)...]
    dot_general x4 -> x0, matrix products: 13 us -> none  [the longest x1 5.46 us: measure(): lax.dot_general(vectors, flat, (((1,), (1,)), ((), ())), preferred_elemen...]
    convert_element_type x2 -> x0, local copies, waits for them, and re-layouts: 6.99 us -> none  [the longest x1 4.97 us: measure(): coupling = jnp.transpose(result, (1, 3, 0, 2)).astype(jnp.bfloat16)]
  transfers between devices with their start and end apart: 2 -> 0, of which waited for: 2 -> 0; matrix products, arithmetic and copies ran while one was open for 0% -> 0% of each run, Pallas kernels for 0% -> 0%
where the time goes in v1:
time: 69.4 us; the launch traced here: 69.2 us
  Pallas kernels  67.8 us (98%)
  local copies, waits for them, and re-layouts  1.42 us (2%)
    pallas_call x1, Pallas kernels, body(): pl.pallas_call(kernel, out_shape=jax.ShapeDtypeStruct((ROWS, SLOTS, NORB)...  67.8 us
    unnamed x1, local copies, waits for them, and re-layouts  1.42 us

profile of v1, /device:TPU:1, one launch (start us, length us, event | category | flops | bytes accessed | tf_op | source)
XLA Modules:
  0.0 69.2 jit_solution(10122834413334426977)
XLA Ops:
  0.0 67.8 %shard_map.73 = bf16[4,8,768]{2,1,0:T(8,128)(2,1)} custom-call(bf16[4,8,768]{2,1,0:T(8,128)(2,1)} %walkers.1, bf16[768,768]{1,0:T(8,128)(2,1)} %one_body.1, f32[8,12]{1,0:T(8,128)} %fields.1, f32[12,768]{1,0:T(8,128)} %field_diag.1, bf16[12,2,8,8,768]{4,3,2,1,0:T(8,128)(2,1)} %bitcast.1, f32[8]{0:T(128)} %weights.1, s32[8]{0:T(128)} %target.1), custom_call_target="tpu_custom_call" | custom-call | tf_op jit(solution)/shard_map/pallas_call | solution.py:288
  67.8 1.4 %copy.9 = bf16[4,8,768]{2,1,0:T(8,128)(2,1)} copy(bf16[4,8,768]{2,1,0:T(8,128)(2,1)} %shard_map.73) | data formatting | bytes 98304

commit v2 on v0

v2 whole, which is shorter than its diff:
```python
import jax
import jax.numpy as jnp
from jax import lax
from jax.experimental import pallas as pl
from jax.experimental.pallas import tpu as pltpu
from jax.sharding import PartitionSpec as P

MESH = pl.DeviceIdType.MESH
F32 = jnp.float32
BF16 = jnp.bfloat16

NZ = 8
NY = 8
SLOTS = 8
HALF = SLOTS // 2
ROWS = 4
QUAD = 4
ZROWS = QUAD * ROWS
NOCC = NZ * ZROWS
NORB = 768
LANES = NORB // 128
VEC = 12
TV = 6
LIVE = 64
ORDER = (2, 1, 3, 0)

RING = (0, 1, 7, 2, 6, 3, 5, 4)


def kernel(
    walkers, one_body, fields, field_diag, chol, weights, target, out,
    XW, WP, GP, S, FI, FD, EP, ER, E, ET, OB, CH, CP, PR, LH, F, XS, XR, T, ZS, ZR, V, U,
    WS, WX, WR,
    loc, es, er, e2s, e2r, ws, wr, ys, yr, cs, cr, gs, gr, xs, xr, rxs, rxr, rzs, rzr,
):
    p = lax.axis_index("grp")
    b = lax.axis_index("blk")
    x_lo, y = p // NY, p % NY
    x_hi, z, c = b // (2 * NZ), (b // 2) % NZ, b % 2
    x_other = x_hi ^ 1

    def at_blk(xh, zz, cc):
        return {"blk": xh * (2 * NZ) + zz * 2 + cc}

    quad = {
        k: at_blk(x_hi ^ 1 if k & 2 else x_hi, z, c ^ 1 if k & 1 else c) for k in (1, 2, 3)
    }
    column = {
        (d, k): at_blk(x_hi, (z + d) % NZ, c ^ k) for d in RING for k in range(2) if d or k
    }
    y_dev = ({"grp": x_lo * NY + (y + 1) % NY}, {"grp": x_lo * NY + (y + NY - 1) % NY})
    x_dev = {"grp": (x_lo ^ 1) * NY + y}
    started = []

    def rcopy(src, dst, s, r, dev):
        return pltpu.make_async_remote_copy(
            src_ref=src, dst_ref=dst, send_sem=s, recv_sem=r, device_id=dev, device_id_type=MESH
        )

    def send(src, dst, s, r, dev):
        copy = rcopy(src, dst, s, r, dev)
        copy.start()
        started.append(copy)

    def arrived(ref, s, r):
        rcopy(ref, ref, s, r, quad[1]).wait_recv()

    local = [
        pltpu.make_async_copy(walkers, XW, loc.at[0]),
        pltpu.make_async_copy(fields, FI, loc.at[1]),
        pltpu.make_async_copy(field_diag, FD, loc.at[2]),
        pltpu.make_async_copy(one_body, OB, loc.at[3]),
        pltpu.make_async_copy(chol, CH.at[0], loc.at[4]),
    ]
    for copy in local:
        copy.start()

    barrier = pltpu.get_barrier_semaphore()
    partners = list(column.values()) + [quad[2], quad[3]] + list(y_dev) + [x_dev]
    for dev in partners:
        pl.semaphore_signal(barrier, inc=1, device_id=dev, device_id_type=MESH)

    local[0].wait()
    low = lax.broadcasted_iota(jnp.int32, (SLOTS, NORB), 0) < HALF
    for r in range(0, ROWS, 2):
        one, two = XW[r].astype(F32), XW[r + 1].astype(F32)
        first = jnp.where(low, one, pltpu.roll(two, HALF, 0))
        second = jnp.where(low, pltpu.roll(one, HALF, 0), two)
        WP[0, r // 2] = first.astype(BF16)
        WP[1, r // 2] = second.astype(BF16)
        GP[x_hi, z, c, r // 2] = jnp.where(c == 0, first, second).astype(BF16)

    local[1].wait()
    local[2].wait()
    part = FI[:, 0:1] * FD[0:1, :]
    for k in range(1, VEC):
        part += FI[:, k : k + 1] * FD[k : k + 1, :]
    EP[0] = part[:HALF]
    EP[1] = part[HALF:]

    own = jnp.float32(0.0)
    for s in range(SLOTS):
        own = own + jnp.where(target[s] < LIVE, weights[s], jnp.float32(0.0))
    WS[...] = jnp.full((8, 128), own, F32)

    pl.semaphore_wait(barrier, len(partners))

    for k in (3, 2, 1):
        send(EP.at[c ^ 1 if k & 1 else c], ER.at[k - 1], es.at[k - 1], er.at[k - 1], quad[k])
    send(WP.at[c], GP.at[x_hi, z, c], xs.at[0, 0], xr.at[0, 0], quad[2])

    def spread(d):
        for k in range(2):
            if d or k:
                send(WP.at[c ^ k], GP.at[x_hi, z, c], gs.at[d, k], gr.at[d, k], column[d, k])

    for d in RING[:5]:
        spread(d)
    send(WS, WX, ws, wr, x_dev)
    send(chol, CH.at[1], cs, cr, quad[1])

    for k in range(3):
        arrived(ER.at[k], es.at[k], er.at[k])
    E[z] = (EP[c] + ER[1]) + (ER[0] + ER[2])
    for d in RING[1:]:
        send(E.at[z], E.at[z], e2s.at[d - 1], e2r.at[d - 1], column[d, 0])
    for d in RING[5:]:
        spread(d)

    def rotate(part, t):
        rows = pl.ds(t * 3 * NOCC, 3 * NOCC)
        flat = CH.at[part].reshape(VEC * NOCC, NORB)
        CP[part, rows, :] = lax.dot_general(
            flat[rows, :], OB[...], (((1,), (1,)), ((), ())), preferred_element_type=F32
        ).astype(BF16)

    def onward(d):
        for k in range(2):
            if d or k:
                ref = GP.at[x_hi, (z + NZ - d) % NZ, c ^ k]
                arrived(ref, gs.at[d, k], gr.at[d, k])
                send(ref, ref, xs.at[d, k], xr.at[d, k], quad[2])

    def weigh(step):
        for way, steps in enumerate((4, 3)):
            if step > 1 and step - 1 <= steps:
                ref = WR.at[(y + NY - step + 1) % NY if way == 0 else (y + step - 1) % NY]
                arrived(ref, ys.at[way, step - 2], yr.at[way, step - 2])
            if step <= steps:
                ref = WR.at[(y + NY - step + 1) % NY if way == 0 else (y + step - 1) % NY]
                send(ref, ref, ys.at[way, step - 1], yr.at[way, step - 1], y_dev[way])

    local[3].wait()
    local[4].wait()
    onward(0)
    rotate(0, 0)
    onward(1)
    onward(7)
    rotate(0, 1)
    onward(2)
    onward(6)
    arrived(WX, ws, wr)
    WR[y] = WS[...] + WX[...]
    weigh(1)
    rotate(0, 2)
    onward(3)
    onward(5)
    rotate(0, 3)
    onward(4)
    weigh(2)
    arrived(CH.at[1], cs, cr)

    for d in RING[1:]:
        arrived(E.at[(z + NZ - d) % NZ], e2s.at[d - 1], e2r.at[d - 1])
    total = E[0]
    for i in range(1, NZ):
        total += E[i]
    grown = jnp.exp(total)
    ET[0:HALF, :] = grown
    ET[HALF:SLOTS, :] = grown

    def scale(xh, d, k):
        zz = (z + NZ - d) % NZ
        base = (xh * 2 * NZ + zz * 2 + (c ^ k)) * ROWS * HALF
        for h in range(2):
            rows = GP[xh, zz, c ^ k, h].astype(F32) * ET[...]
            at = pl.ds(pl.multiple_of(base + h * SLOTS, SLOTS), SLOTS)
            for n in range(LANES):
                S[n, at, :] = rows[:, n * 128 : (n + 1) * 128]

    for i, d in enumerate(RING):
        for k in range(2):
            scale(x_hi, d, k)
        if i % 2:
            rotate(1, i // 2)
    for d in RING:
        for k in range(2):
            arrived(GP.at[x_other, (z + NZ - d) % NZ, c ^ k], xs.at[d, k], xr.at[d, k])
            scale(x_other, d, k)
    weigh(3)
    for w in range(HALF):
        for n in range(LANES):
            PR[w * NOCC : (w + 1) * NOCC, n * 128 : (n + 1) * 128] = S[
                n, pl.ds(w, NOCC, stride=HALF), :
            ].astype(BF16)

    vectors = CH.reshape(2 * VEC * NOCC, NORB)
    rotated = CP.reshape(2 * VEC * NOCC, NORB)

    def compute(pair):
        base = pair * 2 * NOCC
        for t in range(2 * VEC // TV):
            res = lax.dot_general(
                rotated[t * TV * NOCC : (t + 1) * TV * NOCC, :], PR[base : base + 2 * NOCC, :],
                (((1,), (1,)), ((), ())), preferred_element_type=F32,
            ).astype(BF16)
            for g in range(TV):
                for w in range(2):
                    LH[w * NOCC : (w + 1) * NOCC, (t * TV + g) * NOCC : (t * TV + g + 1) * NOCC] = res[
                        g * NOCC : (g + 1) * NOCC, w * NOCC : (w + 1) * NOCC
                    ]
        for n in range(NORB // 256):
            F[base : base + 2 * NOCC, n * 256 : (n + 1) * 256] = jnp.dot(
                LH[...], vectors[:, n * 256 : (n + 1) * 256], preferred_element_type=F32
            )

    def near(k):
        return (z // 2 + k) % (NZ // 2)

    def rows_of(pair, w, xh, zp):
        start = (pair * 2 + w) * NOCC + xh * (NOCC // 2) + zp * ZROWS
        return F[pl.ds(pl.multiple_of(start, ZROWS), ZROWS), :]

    def cross(pair, k):
        for w in range(2):
            XS[pair, k, w] = rows_of(pair, w, x_other, near(k)).astype(BF16)
        send(XS.at[pair, k], XR.at[pair, k], rxs.at[pair, k], rxr.at[pair, k], quad[2])

    def deliver(pair, k):
        arrived(XR.at[pair, k], rxs.at[pair, k], rxr.at[pair, k])
        for w in range(2):
            rows = rows_of(pair, w, x_hi, near(k)) + XR[pair, k, w].astype(F32)
            for n in range(LANES):
                T[pair, k, n, pl.ds(w, ZROWS, stride=2), :] = rows[:, n * 128 : (n + 1) * 128]
        for h in range(2):
            for cc in range(2):
                for n in range(LANES):
                    ZS[pair, k, h, cc, :, n * 128 : (n + 1) * 128] = T[
                        pair, k, n, (h * 2 + cc) * 8 : (h * 2 + cc) * 8 + 8, :
                    ].astype(BF16)
        for t in range(2):
            h = (z % 2) ^ t
            for kc in range(2):
                if k or t or kc:
                    send(
                        ZS.at[pair, k, h, c ^ kc], ZR.at[pair, z, c],
                        rzs.at[pair, k, t, kc], rzr.at[pair, k, t, kc],
                        at_blk(x_hi, near(k) * 2 + h, c ^ kc),
                    )

    def collect(pair):
        for kc in range(2):
            acc = None
            for k in ORDER:
                for t in range(2):
                    zs = ((z // 2 + NZ // 2 - k) % (NZ // 2)) * 2 + ((z % 2) ^ t)
                    if k or t or kc:
                        ref = ZR.at[pair, zs, c ^ kc]
                        arrived(ref, rzs.at[pair, k, t, kc], rzr.at[pair, k, t, kc])
                        rows = ref[...].astype(F32)
                    else:
                        rows = ZS[pair, 0, z % 2, c].astype(F32)
                    acc = rows if acc is None else acc + rows
            at = pl.ds(pl.multiple_of((c ^ kc) * 16 + pair * 8, 8), 8)
            for n in range(LANES):
                V[n, at, :] = acc[:, n * 128 : (n + 1) * 128]

    compute(0)
    for k in ORDER:
        cross(0, k)
    compute(1)
    for k in ORDER:
        cross(1, k)
    weigh(4)
    for pair in range(2):
        for k in ORDER:
            deliver(pair, k)
    weigh(5)
    total = WR[0]
    for i in range(1, NY):
        total += WR[i]
    row = lax.broadcasted_iota(jnp.int32, (8, 128), 0)
    factor = jnp.zeros((8, 128), F32)
    for s in range(SLOTS):
        mine = jnp.where(target[s] < LIVE, weights[s] * LIVE, jnp.float32(0.0))
        factor = jnp.where(row == s, mine, factor)
    factor = factor / total

    for pair in range(2):
        collect(pair)
    for slot in range(SLOTS):
        for n in range(LANES):
            U[n, pl.ds(slot, ROWS, stride=SLOTS), :] = V[
                n, pl.ds((slot // 2) * 8 + slot % 2, ROWS, stride=2), :
            ]
    for r in range(ROWS):
        for n in range(LANES):
            raw = U[n, r * SLOTS : (r + 1) * SLOTS, :].astype(BF16).astype(F32)
            out[r, :, n * 128 : (n + 1) * 128] = (raw * factor).astype(BF16)

    for copy in started:
        copy.wait_send()


def body(walkers, one_body, fields, field_diag, chol, weights, target):
    vmem, sem = pltpu.VMEM, pltpu.SemaphoreType.DMA
    any_, smem = pl.BlockSpec(memory_space=pl.ANY), pl.BlockSpec(memory_space=pltpu.SMEM)
    return pl.pallas_call(
        kernel,
        out_shape=jax.ShapeDtypeStruct((ROWS, SLOTS, NORB), BF16),
        in_specs=[any_] * 5 + [smem] * 2,
        out_specs=pl.BlockSpec(memory_space=pltpu.VMEM),
        scratch_shapes=[
            vmem((ROWS, SLOTS, NORB), BF16),
            vmem((2, 2, SLOTS, NORB), BF16),
            vmem((2, NZ, 2, 2, SLOTS, NORB), BF16),
            vmem((LANES, NOCC * HALF, 128), F32),
            vmem((SLOTS, VEC), F32),
            vmem((VEC, NORB), F32),
            vmem((2, HALF, NORB), F32),
            vmem((3, HALF, NORB), F32),
            vmem((NZ, HALF, NORB), F32),
            vmem((SLOTS, NORB), F32),
            vmem((NORB, NORB), BF16),
            vmem((2, VEC, NOCC, NORB), BF16),
            vmem((2, VEC * NOCC, NORB), BF16),
            vmem((HALF * NOCC, NORB), BF16),
            vmem((2 * NOCC, 2 * VEC * NOCC), BF16),
            vmem((HALF * NOCC, NORB), F32),
            vmem((2, 4, 2, ZROWS, NORB), BF16),
            vmem((2, 4, 2, ZROWS, NORB), BF16),
            vmem((2, 4, LANES, 2 * ZROWS, 128), F32),
            vmem((2, 4, 2, 2, 8, NORB), BF16),
            vmem((2, NZ, 2, 8, NORB), BF16),
            vmem((LANES, 32, 128), F32),
            vmem((LANES, 32, 128), F32),
            vmem((8, 128), F32),
            vmem((8, 128), F32),
            vmem((NY, 8, 128), F32),
            sem((5,)),
            sem((3,)), sem((3,)),
            sem((7,)), sem((7,)),
            sem, sem,
            sem((2, 4)), sem((2, 4)),
            sem, sem,
            sem((NZ, 2)), sem((NZ, 2)),
            sem((NZ, 2)), sem((NZ, 2)),
            sem((2, 4)), sem((2, 4)),
            sem((2, 4, 2, 2)), sem((2, 4, 2, 2)),
        ],
        compiler_params=pltpu.CompilerParams(
            collective_id=0, has_side_effects=True, vmem_limit_bytes=56 * 1024 * 1024
        ),
    )(walkers, one_body, fields, field_diag, chol, weights, target)


def solution(mesh):
    in_specs = (
        P("blk", "grp", None),
        P(),
        P("grp", "blk"),
        P("blk", None),
        P("blk", None, None),
        P("grp"),
        P("grp"),
    )
    out_specs = P("blk", "grp", None)
    return jax.shard_map(body, mesh=mesh, in_specs=in_specs, out_specs=out_specs, check_vma=False)
```

time: 377 us -> 54.2 us (0.14); the launches traced: 372 us -> 54 us
  waiting for transfers between devices: 174 us -> 0 us
  blocking collectives: 162 us -> 0 us
  Pallas kernels: 0 us -> 52.5 us
  between operations: 13.5 us -> 0.01 us
  matrix products: 13 us -> 0 us
  local copies, waits for them, and re-layouts: 7.02 us -> 1.42 us
    psum x2 -> x0, blocking collectives: 162 us -> none  [the longest x1 135 us: body(): exponent = lax.psum(field_part, 'blk')]
    reduce_scatter x1 -> x0, waiting for transfers between devices: 89 us -> none  [measure(): lax.psum_scatter(result.reshape(amount, coupling.shape[1], -1).astype(jnp...]
    all_gather x1 -> x0, waiting for transfers between devices: 84.8 us -> none  [measure(): portion = lax.all_gather(blocks, 'blk', axis=0, tiled=True)]
    pallas_call x0 -> x1, Pallas kernels: none -> 52.5 us  [body(): pl.pallas_call(kernel, out_shape=jax.ShapeDtypeStruct((ROWS, SLOTS, NORB)...]
    dot_general x4 -> x0, matrix products: 13 us -> none  [the longest x1 5.46 us: measure(): lax.dot_general(vectors, flat, (((1,), (1,)), ((), ())), preferred_elemen...]
    convert_element_type x2 -> x0, local copies, waits for them, and re-layouts: 6.99 us -> none  [the longest x1 4.97 us: measure(): coupling = jnp.transpose(result, (1, 3, 0, 2)).astype(jnp.bfloat16)]
  transfers between devices with their start and end apart: 2 -> 0, of which waited for: 2 -> 0; matrix products, arithmetic and copies ran while one was open for 0% -> 0% of each run, Pallas kernels for 0% -> 0%
where the time goes in v2:
time: 54.2 us; the launch traced here: 54 us
  Pallas kernels  52.5 us (97%)
  local copies, waits for them, and re-layouts  1.42 us (3%)
    pallas_call x1, Pallas kernels, body(): pl.pallas_call(kernel, out_shape=jax.ShapeDtypeStruct((ROWS, SLOTS, NORB)...  52.5 us
    unnamed x1, local copies, waits for them, and re-layouts  1.42 us

profile of v2, /device:TPU:1, one launch (start us, length us, event | category | flops | bytes accessed | tf_op | source)
XLA Modules:
  0.0 54.0 jit_solution(8553995323937764138)
XLA Ops:
  0.0 52.5 %shard_map.73 = bf16[4,8,768]{2,1,0:T(8,128)(2,1)} custom-call(bf16[4,8,768]{2,1,0:T(8,128)(2,1)} %walkers.1, bf16[768,768]{1,0:T(8,128)(2,1)} %one_body.1, f32[8,12]{1,0:T(8,128)} %fields.1, f32[12,768]{1,0:T(8,128)} %field_diag.1, bf16[12,128,768]{2,1,0:T(8,128)(2,1)} %chol.1, f32[8]{0:T(128)} %weights.1, s32[8]{0:T(128)} %target.1), custom_call_target="tpu_custom_call" | custom-call | tf_op jit(solution)/shard_map/pallas_call | solution.py:318
  52.6 1.4 %copy.9 = bf16[4,8,768]{2,1,0:T(8,128)(2,1)} copy(bf16[4,8,768]{2,1,0:T(8,128)(2,1)} %shard_map.73) | data formatting | bytes 98304

commit v3 on v2

v3 whole, which is shorter than its diff:
```python
import jax
import jax.numpy as jnp
from jax import lax
from jax.experimental import pallas as pl
from jax.experimental.pallas import tpu as pltpu
from jax.sharding import PartitionSpec as P

MESH = pl.DeviceIdType.MESH
F32 = jnp.float32
BF16 = jnp.bfloat16

NZ = 8
NY = 8
SLOTS = 8
HALF = SLOTS // 2
ROWS = 4
QUAD = 4
ZROWS = QUAD * ROWS
NOCC = NZ * ZROWS
NORB = 768
LANES = NORB // 128
VEC = 12
TV = 6
LIVE = 64

RING = (0, 1, 7, 2, 6, 3, 5, 4)


def kernel(
    walkers, one_body, fields, field_diag, chol, weights, target, out,
    XW, WP, GP, S, FI, FD, EP, ER, E, ET, OB, CH, CP, PR, LH, F, XS, XR, T, ZS, ZR, V, U,
    WG, TG, WS, WX, WR,
    loc, es, er, e2s, e2r, ws, wr, ys, yr, cs, cr, gs, gr, xs, xr, rxs, rxr, rzs, rzr, ready,
):
    p = lax.axis_index("grp")
    b = lax.axis_index("blk")
    x_lo, y = p // NY, p % NY
    x_hi, z, c = b // (2 * NZ), (b // 2) % NZ, b % 2
    x_other = x_hi ^ 1

    def at_blk(xh, zz, cc):
        return {"blk": xh * (2 * NZ) + zz * 2 + cc}

    quad = {
        k: at_blk(x_hi ^ 1 if k & 2 else x_hi, z, c ^ 1 if k & 1 else c) for k in (1, 2, 3)
    }
    y_dev = ({"grp": x_lo * NY + (y + 1) % NY}, {"grp": x_lo * NY + (y + NY - 1) % NY})
    x_dev = {"grp": (x_lo ^ 1) * NY + y}
    started = []

    def rcopy(src, dst, s, r, dev):
        return pltpu.make_async_remote_copy(
            src_ref=src, dst_ref=dst, send_sem=s, recv_sem=r, device_id=dev, device_id_type=MESH
        )

    def send(src, dst, s, r, dev, when=None):
        copy = rcopy(src, dst, s, r, dev)
        if when is None:
            copy.start()
        else:
            pl.when(when)(lambda: copy.start())
        started.append((when, copy))

    def arrived(ref, s, r, when=None):
        copy = rcopy(ref, ref, s, r, quad[1])
        if when is None:
            copy.wait_recv()
        else:
            pl.when(when)(lambda: copy.wait_recv())

    local = [
        pltpu.make_async_copy(walkers, XW, loc.at[0]),
        pltpu.make_async_copy(fields, FI, loc.at[1]),
        pltpu.make_async_copy(field_diag, FD, loc.at[2]),
        pltpu.make_async_copy(one_body, OB, loc.at[3]),
        pltpu.make_async_copy(chol, CH.at[0], loc.at[4]),
        pltpu.make_async_copy(weights, WG, loc.at[5]),
        pltpu.make_async_copy(target, TG, loc.at[6]),
    ]
    for copy in local:
        copy.start()

    def say(sem, zz, k):
        pl.semaphore_signal(sem, inc=1, device_id=at_blk(x_hi, zz, c ^ k), device_id_type=MESH)

    barrier = pltpu.get_barrier_semaphore()
    always = list(quad.values()) + list(y_dev) + [x_dev]
    for dev in always:
        pl.semaphore_signal(barrier, inc=1, device_id=dev, device_id_type=MESH)
    for zz in range(1, NZ):

        @pl.when(zz > z)
        def _(zz=zz):
            say(barrier, zz, 0)
            say(barrier, zz, 1)

    pl.semaphore_wait(barrier, len(always) + 2 * z)
    for zz in range(NZ - 1):

        @pl.when(zz < z)
        def _(zz=zz):
            say(ready.at[z, 0], zz, 0)
            say(ready.at[z, 1], zz, 1)

    local[0].wait()
    low = lax.broadcasted_iota(jnp.int32, (SLOTS, NORB), 0) < HALF
    for r in range(0, ROWS, 2):
        one, two = XW[r].astype(F32), XW[r + 1].astype(F32)
        first = jnp.where(low, one, pltpu.roll(two, HALF, 0))
        second = jnp.where(low, pltpu.roll(one, HALF, 0), two)
        WP[0, r // 2] = first.astype(BF16)
        WP[1, r // 2] = second.astype(BF16)
        GP[x_hi, z, c, r // 2] = jnp.where(c == 0, first, second).astype(BF16)

    def spread(zz, when):
        for k in range(2):
            send(
                WP.at[c ^ k], GP.at[x_hi, z, c], gs.at[zz, k], gr.at[z, k],
                at_blk(x_hi, zz, c ^ k), when,
            )

    send(WP.at[c], GP.at[x_hi, z, c], xs.at[z, 0], xr.at[z, 0], quad[2])
    for d in RING[1:]:
        spread((z + d) % NZ, (z + d) % NZ < z)
    send(WP.at[c ^ 1], GP.at[x_hi, z, c], gs.at[z, 1], gr.at[z, 1], quad[1])

    local[1].wait()
    local[2].wait()
    part = FI[:, 0:1] * FD[0:1, :]
    for k in range(1, VEC):
        part += FI[:, k : k + 1] * FD[k : k + 1, :]
    EP[0] = part[:HALF]
    EP[1] = part[HALF:]
    for k in (3, 2, 1):
        send(EP.at[c ^ 1 if k & 1 else c], ER.at[k - 1], es.at[k - 1], er.at[k - 1], quad[k])

    local[5].wait()
    local[6].wait()
    live = jnp.where(TG[...] < LIVE, WG[...], jnp.float32(0.0))
    same = lax.broadcasted_iota(jnp.int32, (SLOTS, SLOTS), 0) == lax.broadcasted_iota(
        jnp.int32, (SLOTS, SLOTS), 1
    )
    mine = jnp.sum(
        jnp.where(same, jnp.broadcast_to(live, (SLOTS, SLOTS)), 0.0), axis=1, keepdims=True
    )
    WS[...] = jnp.broadcast_to(jnp.sum(live, axis=1, keepdims=True), (8, 128))
    send(chol, CH.at[1], cs, cr, quad[1])
    send(WS, WX, ws, wr, x_dev)

    def rotate(part, t):
        rows = pl.ds(t * 3 * NOCC, 3 * NOCC)
        flat = CH.at[part].reshape(VEC * NOCC, NORB)
        CP[part, rows, :] = lax.dot_general(
            flat[rows, :], OB[...], (((1,), (1,)), ((), ())), preferred_element_type=F32
        ).astype(BF16)

    def onward(zz):
        for k in range(2):
            when = None if k else z != zz
            ref = GP.at[x_hi, zz, c ^ k]
            arrived(ref, gs.at[zz, k], gr.at[zz, k], when)
            send(ref, ref, xs.at[zz, k], xr.at[zz, k], quad[2], when)

    def weigh(step):
        for way, steps in enumerate((4, 3)):
            if step > 1 and step - 1 <= steps:
                ref = WR.at[(y + NY - step + 1) % NY if way == 0 else (y + step - 1) % NY]
                arrived(ref, ys.at[way, step - 2], yr.at[way, step - 2])
            if step <= steps:
                ref = WR.at[(y + NY - step + 1) % NY if way == 0 else (y + step - 1) % NY]
                send(ref, ref, ys.at[way, step - 1], yr.at[way, step - 1], y_dev[way])

    for j in range(1, NZ):
        later = z + j < NZ
        zz = jnp.minimum(z + j, NZ - 1)

        @pl.when(later)
        def _(zz=zz):
            pl.semaphore_wait(ready.at[zz, 0], 1)
            pl.semaphore_wait(ready.at[zz, 1], 1)

        spread(zz, later)
        if j == 1:
            local[3].wait()
            local[4].wait()
        if j == 3:
            for k in range(3):
                arrived(ER.at[k], es.at[k], er.at[k])
            E[z] = (EP[c] + ER[1]) + (ER[0] + ER[2])
            for d in RING[1:]:
                other = (z + d) % NZ
                send(
                    E.at[z], E.at[z], e2s.at[other], e2r.at[z],
                    at_blk(x_hi, other, c), other < z + j + 1,
                )
        if j > 3:
            send(E.at[z], E.at[z], e2s.at[zz], e2r.at[z], at_blk(x_hi, zz, c), later)
            onward(j - 4)
        if j == 5:
            arrived(CH.at[1], cs, cr)
        rotate(j // 5, (j - 1) % 4)
    rotate(1, 3)
    arrived(WX, ws, wr)
    WR[y] = WS[...] + WX[...]
    weigh(1)
    for zz in range(4, NZ):
        onward(zz)
    for zz in range(NZ):
        arrived(E.at[zz], e2s.at[zz], e2r.at[zz], z != zz)
    total = E[0]
    for i in range(1, NZ):
        total += E[i]
    grown = jnp.exp(total)
    ET[0:HALF, :] = grown
    ET[HALF:SLOTS, :] = grown

    def scale(xh, zz, k):
        base = (xh * 2 * NZ + zz * 2 + (c ^ k)) * ROWS * HALF
        for h in range(2):
            rows = GP[xh, zz, c ^ k, h].astype(F32) * ET[...]
            at = pl.ds(pl.multiple_of(base + h * SLOTS, SLOTS), SLOTS)
            for n in range(LANES):
                S[n, at, :] = rows[:, n * 128 : (n + 1) * 128]

    def gathered(xh):
        for w in range(HALF):
            at = pl.ds(pl.multiple_of(w * NOCC + xh * (NOCC // 2), NOCC // 2), NOCC // 2)
            for n in range(LANES):
                PR[at, n * 128 : (n + 1) * 128] = S[
                    n, pl.ds(xh * (NOCC * HALF // 2) + w, NOCC // 2, stride=HALF), :
                ].astype(BF16)

    for zz in range(NZ):
        for k in range(2):
            scale(x_hi, zz, k)
    gathered(x_hi)
    for zz in range(NZ):
        for k in range(2):
            arrived(GP.at[x_other, zz, c ^ k], xs.at[zz, k], xr.at[zz, k])
            scale(x_other, zz, k)
    gathered(x_other)
    weigh(2)

    vectors = CH.reshape(2 * VEC * NOCC, NORB)
    rotated = CP.reshape(2 * VEC * NOCC, NORB)

    def compute(pair):
        base = pair * 2 * NOCC
        for t in range(2 * VEC // TV):
            res = lax.dot_general(
                rotated[t * TV * NOCC : (t + 1) * TV * NOCC, :], PR[base : base + 2 * NOCC, :],
                (((1,), (1,)), ((), ())), preferred_element_type=F32,
            ).astype(BF16)
            for g in range(TV):
                for w in range(2):
                    LH[w * NOCC : (w + 1) * NOCC, (t * TV + g) * NOCC : (t * TV + g + 1) * NOCC] = res[
                        g * NOCC : (g + 1) * NOCC, w * NOCC : (w + 1) * NOCC
                    ]
        for n in range(NORB // 256):
            F[base : base + 2 * NOCC, n * 256 : (n + 1) * 256] = jnp.dot(
                LH[...], vectors[:, n * 256 : (n + 1) * 256], preferred_element_type=F32
            )

    def rows_of(pair, w, xh, zp):
        start = (pair * 2 + w) * NOCC + xh * (NOCC // 2) + zp * ZROWS
        return F[pl.ds(pl.multiple_of(start, ZROWS), ZROWS), :]

    def cross(pair, zp):
        for w in range(2):
            XS[pair, zp, w] = rows_of(pair, w, x_other, zp).astype(BF16)
        send(XS.at[pair, zp], XR.at[pair, zp], rxs.at[pair, zp], rxr.at[pair, zp], quad[2])

    def deliver(pair, zp):
        arrived(XR.at[pair, zp], rxs.at[pair, zp], rxr.at[pair, zp])
        for w in range(2):
            rows = rows_of(pair, w, x_hi, zp) + XR[pair, zp, w].astype(F32)
            for n in range(LANES):
                T[pair, zp, n, pl.ds(w, ZROWS, stride=2), :] = rows[:, n * 128 : (n + 1) * 128]
        for h in range(2):
            zz = zp * 2 + h
            for cc in range(2):
                for n in range(LANES):
                    ZS[pair, zz, cc, :, n * 128 : (n + 1) * 128] = T[
                        pair, zp, n, (h * 2 + cc) * 8 : (h * 2 + cc) * 8 + 8, :
                    ].astype(BF16)
        for h in range(2):
            zz = zp * 2 + h
            for kc in range(2):
                send(
                    ZS.at[pair, zz, c ^ kc], ZR.at[pair, z, c],
                    rzs.at[pair, zz, kc], rzr.at[pair, z, kc],
                    at_blk(x_hi, zz, c ^ kc), None if kc else z != zz,
                )

    def collect(pair):
        ZR[pair, z, c] = ZS[pair, z, c]
        for kc in range(2):
            acc = None
            for zs in range(NZ):
                ref = ZR.at[pair, zs, c ^ kc]
                arrived(ref, rzs.at[pair, zs, kc], rzr.at[pair, zs, kc], None if kc else z != zs)
                rows = ref[...].astype(F32)
                acc = rows if acc is None else acc + rows
            at = pl.ds(pl.multiple_of((c ^ kc) * 16 + pair * 8, 8), 8)
            for n in range(LANES):
                V[n, at, :] = acc[:, n * 128 : (n + 1) * 128]

    compute(0)
    for zp in range(NZ // 2):
        cross(0, zp)
    weigh(3)
    compute(1)
    for zp in range(NZ // 2):
        cross(1, zp)
    for pair in range(2):
        for zp in range(NZ // 2):
            deliver(pair, zp)
        weigh(4 + pair)
    total = WR[0]
    for i in range(1, NY):
        total += WR[i]
    factor = jnp.broadcast_to(mine * LIVE, (8, 128)) / total

    for pair in range(2):
        collect(pair)
    for slot in range(SLOTS):
        for n in range(LANES):
            U[n, pl.ds(slot, ROWS, stride=SLOTS), :] = V[
                n, pl.ds((slot // 2) * 8 + slot % 2, ROWS, stride=2), :
            ]
    for r in range(ROWS):
        for n in range(LANES):
            raw = U[n, r * SLOTS : (r + 1) * SLOTS, :].astype(BF16).astype(F32)
            out[r, :, n * 128 : (n + 1) * 128] = (raw * factor).astype(BF16)

    for when, copy in started:
        if when is None:
            copy.wait_send()
        else:
            pl.when(when)(lambda copy=copy: copy.wait_send())


def body(walkers, one_body, fields, field_diag, chol, weights, target):
    vmem, sem = pltpu.VMEM, pltpu.SemaphoreType.DMA
    any_ = pl.BlockSpec(memory_space=pl.ANY)
    return pl.pallas_call(
        kernel,
        out_shape=pltpu.VMEM((ROWS, SLOTS, NORB), BF16),
        in_specs=[any_] * 7,
        out_specs=pl.BlockSpec(memory_space=pltpu.VMEM),
        scratch_shapes=[
            vmem((ROWS, SLOTS, NORB), BF16),
            vmem((2, 2, SLOTS, NORB), BF16),
            vmem((2, NZ, 2, 2, SLOTS, NORB), BF16),
            vmem((LANES, NOCC * HALF, 128), F32),
            vmem((SLOTS, VEC), F32),
            vmem((VEC, NORB), F32),
            vmem((2, HALF, NORB), F32),
            vmem((3, HALF, NORB), F32),
            vmem((NZ, HALF, NORB), F32),
            vmem((SLOTS, NORB), F32),
            vmem((NORB, NORB), BF16),
            vmem((2, VEC, NOCC, NORB), BF16),
            vmem((2, VEC * NOCC, NORB), BF16),
            vmem((HALF * NOCC, NORB), BF16),
            vmem((2 * NOCC, 2 * VEC * NOCC), BF16),
            vmem((HALF * NOCC, NORB), F32),
            vmem((2, 4, 2, ZROWS, NORB), BF16),
            vmem((2, 4, 2, ZROWS, NORB), BF16),
            vmem((2, 4, LANES, 2 * ZROWS, 128), F32),
            vmem((2, NZ, 2, 8, NORB), BF16),
            vmem((2, NZ, 2, 8, NORB), BF16),
            vmem((LANES, 32, 128), F32),
            vmem((LANES, 32, 128), F32),
            vmem((1, SLOTS), F32),
            vmem((1, SLOTS), jnp.int32),
            vmem((8, 128), F32),
            vmem((8, 128), F32),
            vmem((NY, 8, 128), F32),
            sem((7,)),
            sem((3,)), sem((3,)),
            sem((NZ,)), sem((NZ,)),
            sem, sem,
            sem((2, 4)), sem((2, 4)),
            sem, sem,
            sem((NZ, 2)), sem((NZ, 2)),
            sem((NZ, 2)), sem((NZ, 2)),
            sem((2, 4)), sem((2, 4)),
            sem((2, NZ, 2)), sem((2, NZ, 2)),
            pltpu.SemaphoreType.REGULAR((NZ, 2)),
        ],
        compiler_params=pltpu.CompilerParams(
            collective_id=0, has_side_effects=True, vmem_limit_bytes=56 * 1024 * 1024
        ),
    )(
        walkers, one_body, fields, field_diag, chol,
        weights.reshape(1, SLOTS), target.reshape(1, SLOTS),
    )


def solution(mesh):
    in_specs = (
        P("blk", "grp", None),
        P(),
        P("grp", "blk"),
        P("blk", None),
        P("blk", None, None),
        P("grp"),
        P("grp"),
    )
    out_specs = P("blk", "grp", None)
    return jax.shard_map(body, mesh=mesh, in_specs=in_specs, out_specs=out_specs, check_vma=False)
```

time: 54.2 us -> 57.1 us (1.054)
  Pallas kernels: 52.5 us -> 56.4 us
  local copies, waits for them, and re-layouts: 1.42 us -> 0.62 us
    pallas_call x1, Pallas kernels: 52.5 us -> 56.4 us  [body(): pl.pallas_call(kernel, out_shape=pltpu.VMEM((ROWS, SLOTS, NORB), BF16), i...]
    unnamed x1, local copies, waits for them, and re-layouts: 1.42 us -> 0.62 us
where the time goes in v3:
time: 57.1 us; the launch traced here: 57 us
  Pallas kernels  56.4 us (99%)
  local copies, waits for them, and re-layouts  0.62 us (1%)
    pallas_call x1, Pallas kernels, body(): pl.pallas_call(kernel, out_shape=pltpu.VMEM((ROWS, SLOTS, NORB), BF16), i...  56.4 us

profile of v3, /device:TPU:1, one launch (start us, length us, event | category | flops | bytes accessed | tf_op | source)
XLA Modules:
  0.0 57.0 jit_solution(7213778153172519408)
XLA Ops:
  0.0 56.4 %shard_map.73 = bf16[4,8,768]{2,1,0:T(8,128)(2,1)S(1)} custom-call(bf16[4,8,768]{2,1,0:T(8,128)(2,1)} %walkers.1, bf16[768,768]{1,0:T(8,128)(2,1)} %one_body.1, f32[8,12]{1,0:T(8,128)} %fields.1, f32[12,768]{1,0:T(8,128)} %field_diag.1, bf16[12,128,768]{2,1,0:T(8,128)(2,1)} %chol.1, f32[1,8]{1,0:T(1,128)} %bitcast.2, s32[1,8]{1,0:T(1,128)} %bitcast.3), custom_call_target="tpu_custom_call" | custom-call | tf_op jit(solution)/shard_map/pallas_call | solution.py:346
  56.4 0.6 %copy.9 = bf16[4,8,768]{2,1,0:T(8,128)(2,1)} copy(bf16[4,8,768]{2,1,0:T(8,128)(2,1)S(1)} %shard_map.73) | data formatting | bytes 98304

commit v4 on v2

--- a/solution.py
+++ b/solution.py
@@ -317,7 +317,7 @@
     any_, smem = pl.BlockSpec(memory_space=pl.ANY), pl.BlockSpec(memory_space=pltpu.SMEM)
     return pl.pallas_call(
         kernel,
-        out_shape=jax.ShapeDtypeStruct((ROWS, SLOTS, NORB), BF16),
+        out_shape=pltpu.VMEM((ROWS, SLOTS, NORB), BF16),
         in_specs=[any_] * 5 + [smem] * 2,
         out_specs=pl.BlockSpec(memory_space=pltpu.VMEM),
         scratch_shapes=[

time: 54.2 us -> 52.7 us (0.972)
  local copies, waits for them, and re-layouts: 1.42 us -> 0.62 us
  Pallas kernels: 52.5 us -> 51.9 us
    unnamed x1, local copies, waits for them, and re-layouts: 1.42 us -> 0.62 us
    pallas_call x1, Pallas kernels: 52.5 us -> 51.9 us  [body(): pl.pallas_call(kernel, out_shape=pltpu.VMEM((ROWS, SLOTS, NORB), BF16), i...]
where the time goes in v4:
time: 52.7 us; the launch traced here: 52.6 us
  Pallas kernels  51.9 us (98%)
  local copies, waits for them, and re-layouts  0.62 us (1%)
    pallas_call x1, Pallas kernels, body(): pl.pallas_call(kernel, out_shape=pltpu.VMEM((ROWS, SLOTS, NORB), BF16), i...  51.9 us

profile of v4, /device:TPU:1, one launch (start us, length us, event | category | flops | bytes accessed | tf_op | source)
XLA Modules:
  0.0 52.6 jit_solution(6595874994542925410)
XLA Ops:
  0.0 51.9 %shard_map.73 = bf16[4,8,768]{2,1,0:T(8,128)(2,1)S(1)} custom-call(bf16[4,8,768]{2,1,0:T(8,128)(2,1)} %walkers.1, bf16[768,768]{1,0:T(8,128)(2,1)} %one_body.1, f32[8,12]{1,0:T(8,128)} %fields.1, f32[12,768]{1,0:T(8,128)} %field_diag.1, bf16[12,128,768]{2,1,0:T(8,128)(2,1)} %chol.1, f32[8]{0:T(128)} %weights.1, s32[8]{0:T(128)} %target.1), custom_call_target="tpu_custom_call" | custom-call | tf_op jit(solution)/shard_map/pallas_call | solution.py:318
  51.9 0.6 %copy.9 = bf16[4,8,768]{2,1,0:T(8,128)(2,1)} copy(bf16[4,8,768]{2,1,0:T(8,128)(2,1)S(1)} %shard_map.73) | data formatting | bytes 98304

commit v5 on v4

--- a/solution.py
+++ b/solution.py
@@ -30,8 +30,8 @@
 def kernel(
     walkers, one_body, fields, field_diag, chol, weights, target, out,
     XW, WP, GP, S, FI, FD, EP, ER, E, ET, OB, CH, CP, PR, LH, F, XS, XR, T, ZS, ZR, V, U,
-    WS, WX, WR,
-    loc, es, er, e2s, e2r, ws, wr, ys, yr, cs, cr, gs, gr, xs, xr, rxs, rxr, rzs, rzr,
+    WG, TG, WS, WX, WR,
+    loc, es, er, e2s, e2r, ws, wr, ys, yr, cs, cr, gs, gr, xs, xr, rxs, rxr, rzs, rzr, fs, fr,
 ):
     p = lax.axis_index("grp")
     b = lax.axis_index("blk")
@@ -71,6 +71,8 @@
         pltpu.make_async_copy(field_diag, FD, loc.at[2]),
         pltpu.make_async_copy(one_body, OB, loc.at[3]),
         pltpu.make_async_copy(chol, CH.at[0], loc.at[4]),
+        pltpu.make_async_copy(weights, WG, loc.at[5]),
+        pltpu.make_async_copy(target, TG, loc.at[6]),
     ]
     for copy in local:
         copy.start()
@@ -98,10 +100,16 @@
     EP[0] = part[:HALF]
     EP[1] = part[HALF:]
 
-    own = jnp.float32(0.0)
-    for s in range(SLOTS):
-        own = own + jnp.where(target[s] < LIVE, weights[s], jnp.float32(0.0))
-    WS[...] = jnp.full((8, 128), own, F32)
+    local[5].wait()
+    local[6].wait()
+    live = jnp.where(TG[...] < LIVE, WG[...], jnp.float32(0.0))
+    same = lax.broadcasted_iota(jnp.int32, (SLOTS, SLOTS), 0) == lax.broadcasted_iota(
+        jnp.int32, (SLOTS, SLOTS), 1
+    )
+    mine = jnp.sum(
+        jnp.where(same, jnp.broadcast_to(live, (SLOTS, SLOTS)), 0.0), axis=1, keepdims=True
+    )
+    WS[...] = jnp.broadcast_to(jnp.sum(live, axis=1, keepdims=True), (8, 128))
 
     pl.semaphore_wait(barrier, len(partners))
 
@@ -116,16 +124,14 @@
 
     for d in RING[:5]:
         spread(d)
+    send(chol, CH.at[1], cs, cr, quad[1])
     send(WS, WX, ws, wr, x_dev)
-    send(chol, CH.at[1], cs, cr, quad[1])
 
     for k in range(3):
         arrived(ER.at[k], es.at[k], er.at[k])
     E[z] = (EP[c] + ER[1]) + (ER[0] + ER[2])
     for d in RING[1:]:
         send(E.at[z], E.at[z], e2s.at[d - 1], e2r.at[d - 1], column[d, 0])
-    for d in RING[5:]:
-        spread(d)
 
     def rotate(part, t):
         rows = pl.ds(t * 3 * NOCC, 3 * NOCC)
@@ -150,23 +156,38 @@
                 ref = WR.at[(y + NY - step + 1) % NY if way == 0 else (y + step - 1) % NY]
                 send(ref, ref, ys.at[way, step - 1], yr.at[way, step - 1], y_dev[way])
 
+    def crossed(d, k):
+        ref = GP.at[x_other, (z + NZ - d) % NZ, c ^ k]
+        if d == 4:
+            arrived(ref, fs.at[k], fr.at[k])
+        else:
+            arrived(ref, xs.at[d, k], xr.at[d, k])
+
+    onward(0)
+    spread(3)
+    spread(5)
     local[3].wait()
     local[4].wait()
-    onward(0)
-    rotate(0, 0)
     onward(1)
     onward(7)
-    rotate(0, 1)
+    spread(4)
+    for k in range(2):
+        crossed(0, k)
+        ref = GP.at[x_other, z, c ^ k]
+        send(ref, ref, fs.at[k], fr.at[k], column[4, 0])
+    rotate(0, 0)
     onward(2)
     onward(6)
     arrived(WX, ws, wr)
     WR[y] = WS[...] + WX[...]
     weigh(1)
+    rotate(0, 1)
     rotate(0, 2)
     onward(3)
     onward(5)
+    for k in range(2):
+        arrived(GP.at[x_hi, (z + 4) % NZ, c ^ k], gs.at[4, k], gr.at[4, k])
     rotate(0, 3)
-    onward(4)
     weigh(2)
     arrived(CH.at[1], cs, cr)
 
@@ -188,21 +209,27 @@
             for n in range(LANES):
                 S[n, at, :] = rows[:, n * 128 : (n + 1) * 128]
 
+    def gathered(xh):
+        for w in range(HALF):
+            at = pl.ds(pl.multiple_of(w * NOCC + xh * (NOCC // 2), NOCC // 2), NOCC // 2)
+            for n in range(LANES):
+                PR[at, n * 128 : (n + 1) * 128] = S[
+                    n, pl.ds(xh * (NOCC * HALF // 2) + w, NOCC // 2, stride=HALF), :
+                ].astype(BF16)
+
     for i, d in enumerate(RING):
         for k in range(2):
             scale(x_hi, d, k)
         if i % 2:
             rotate(1, i // 2)
+    gathered(x_hi)
     for d in RING:
         for k in range(2):
-            arrived(GP.at[x_other, (z + NZ - d) % NZ, c ^ k], xs.at[d, k], xr.at[d, k])
+            if d:
+                crossed(d, k)
             scale(x_other, d, k)
+    gathered(x_other)
     weigh(3)
-    for w in range(HALF):
-        for n in range(LANES):
-            PR[w * NOCC : (w + 1) * NOCC, n * 128 : (n + 1) * 128] = S[
-                n, pl.ds(w, NOCC, stride=HALF), :
-            ].astype(BF16)
 
     vectors = CH.reshape(2 * VEC * NOCC, NORB)
     rotated = CP.reshape(2 * VEC * NOCC, NORB)
@@ -289,12 +316,7 @@
     total = WR[0]
     for i in range(1, NY):
         total += WR[i]
-    row = lax.broadcasted_iota(jnp.int32, (8, 128), 0)
-    factor = jnp.zeros((8, 128), F32)
-    for s in range(SLOTS):
-        mine = jnp.where(target[s] < LIVE, weights[s] * LIVE, jnp.float32(0.0))
-        factor = jnp.where(row == s, mine, factor)
-    factor = factor / total
+    factor = jnp.broadcast_to(mine * LIVE, (8, 128)) / total
 
     for pair in range(2):
         collect(pair)
@@ -314,11 +336,11 @@
 
 def body(walkers, one_body, fields, field_diag, chol, weights, target):
     vmem, sem = pltpu.VMEM, pltpu.SemaphoreType.DMA
-    any_, smem = pl.BlockSpec(memory_space=pl.ANY), pl.BlockSpec(memory_space=pltpu.SMEM)
+    any_ = pl.BlockSpec(memory_space=pl.ANY)
     return pl.pallas_call(
         kernel,
         out_shape=pltpu.VMEM((ROWS, SLOTS, NORB), BF16),
-        in_specs=[any_] * 5 + [smem] * 2,
+        in_specs=[any_] * 7,
         out_specs=pl.BlockSpec(memory_space=pltpu.VMEM),
         scratch_shapes=[
             vmem((ROWS, SLOTS, NORB), BF16),
@@ -344,10 +366,12 @@
             vmem((2, NZ, 2, 8, NORB), BF16),
             vmem((LANES, 32, 128), F32),
             vmem((LANES, 32, 128), F32),
+            vmem((1, SLOTS), F32),
+            vmem((1, SLOTS), jnp.int32),
             vmem((8, 128), F32),
             vmem((8, 128), F32),
             vmem((NY, 8, 128), F32),
-            sem((5,)),
+            sem((7,)),
             sem((3,)), sem((3,)),
             sem((7,)), sem((7,)),
             sem, sem,
@@ -357,11 +381,15 @@
             sem((NZ, 2)), sem((NZ, 2)),
             sem((2, 4)), sem((2, 4)),
             sem((2, 4, 2, 2)), sem((2, 4, 2, 2)),
+            sem((2,)), sem((2,)),
         ],
         compiler_params=pltpu.CompilerParams(
             collective_id=0, has_side_effects=True, vmem_limit_bytes=56 * 1024 * 1024
         ),
-    )(walkers, one_body, fields, field_diag, chol, weights, target)
+    )(
+        walkers, one_body, fields, field_diag, chol,
+        weights.reshape(1, SLOTS), target.reshape(1, SLOTS),
+    )
 
 
 def solution(mesh):

time: 52.7 us -> 54.2 us (1.028)
  Pallas kernels: 51.9 us -> 53.4 us
    pallas_call x1, Pallas kernels: 51.9 us -> 53.4 us  [body(): pl.pallas_call(kernel, out_shape=pltpu.VMEM((ROWS, SLOTS, NORB), BF16), i...]
where the time goes in v5:
time: 54.2 us; the launch traced here: 54.1 us
  Pallas kernels  53.4 us (99%)
  local copies, waits for them, and re-layouts  0.62 us (1%)
    pallas_call x1, Pallas kernels, body(): pl.pallas_call(kernel, out_shape=pltpu.VMEM((ROWS, SLOTS, NORB), BF16), i...  53.4 us

profile of v5, /device:TPU:1, one launch (start us, length us, event | category | flops | bytes accessed | tf_op | source)
XLA Modules:
  0.0 54.1 jit_solution(13717368518209469420)
XLA Ops:
  0.0 53.4 %shard_map.73 = bf16[4,8,768]{2,1,0:T(8,128)(2,1)S(1)} custom-call(bf16[4,8,768]{2,1,0:T(8,128)(2,1)} %walkers.1, bf16[768,768]{1,0:T(8,128)(2,1)} %one_body.1, f32[8,12]{1,0:T(8,128)} %fields.1, f32[12,768]{1,0:T(8,128)} %field_diag.1, bf16[12,128,768]{2,1,0:T(8,128)(2,1)} %chol.1, f32[1,8]{1,0:T(1,128)} %bitcast.2, s32[1,8]{1,0:T(1,128)} %bitcast.3), custom_call_target="tpu_custom_call" | custom-call | tf_op jit(solution)/shard_map/pallas_call | solution.py:340
  53.4 0.6 %copy.9 = bf16[4,8,768]{2,1,0:T(8,128)(2,1)} copy(bf16[4,8,768]{2,1,0:T(8,128)(2,1)S(1)} %shard_map.73) | data formatting | bytes 98304
